TPU v7x, 32 devices: a whole 2x2x4 slice. The times are simulated.
32 devices in a mesh: row: 4 (over z), col: 8 (over y, x, core).
Axes of the slice: x: 2, y: 2, z: 4, core: 2. Of those that a mesh axis runs over, the one named last changes fastest.
Arguments:
- panel_block: bfloat16 [3584, 1024], P(('row', 'col')), may hold values from -1.5 to 1.5
- diag_inverse: bfloat16 [2, 512, 512], replicated
- trailing: bfloat16 [3584, 3584], P('row', 'col'), may hold values from -6 to 6
Outputs:
- factor_panel: bfloat16 [3584, 1024], P(('row', 'col'))
- updated: bfloat16 [3584, 3584], P('row', 'col')
All inputs are finite; a program needn't handle non-finite values.
Results may differ from a plain program's by a relative error of at most 0.0054.
Values may be sent and summed in bfloat16 or wider, within the bound.
No kernel may reach another device: no remote copies, remote signals or barrier semaphores. Data moves between devices by JAX's collectives and lax.ppermute only.
A program may use at most 128 MiB of HBM per device.

v0:
```python
import jax
import jax.numpy as jnp
from jax import lax
from jax.sharding import PartitionSpec as P

NB = 512
PANELS = 2


def body(panel_block, diag_inverse, trailing):
    pieces = []
    for panel in range(PANELS):
        columns = panel_block[:, panel * NB : (panel + 1) * NB]
        pieces.append(
            jnp.dot(
                columns, jnp.tril(diag_inverse[panel]).T, preferred_element_type=jnp.float32
            ).astype(jnp.bfloat16)
        )
    factor = jnp.concatenate(pieces, axis=1)
    column_block = lax.all_gather(factor, "row", axis=0, tiled=True)
    product = lax.dot_general(
        lax.all_gather(factor, "col", axis=0, tiled=True),
        column_block,
        (((1,), (1,)), ((), ())),
        preferred_element_type=jnp.float32,
    )
    updated = (trailing.astype(jnp.float32) - product).astype(jnp.bfloat16)
    return (factor, updated)


def solution(mesh):
    placed = (P(("row", "col"), None), P(), P("row", "col"))
    return jax.shard_map(
        body,
        mesh=mesh,
        in_specs=placed,
        out_specs=(P(("row", "col"), None), P("row", "col")),
        check_vma=False,
    )
```

profile of v0, /device:TPU:0, one launch (start us, length us, event | category | flops | bytes accessed | tf_op | source)
XLA Modules:
  0.0 50.7 jit_solution(15420570001928043518)
XLA Ops:
  7.2 0.0 all-gather.2.cloned.1.call-start
  7.2 1.3 %fusion.1 = bf16[112,512]{1,0:T(8,128)(2,1)S(1)} fusion(bf16[2,512,512]{2,1,0:T(8,128)(2,1)} %param.4, bf16[112,1024]{1,0:T(8,128)(2,1)} %param.3), kind=kOutput, calls=%fused_computation.4 | convolution fusion | flops 59301888 | bytes 753664 | tf_op jit(solution)/shard_map/dot_general | solution.py:15
  8.6 0.0 copy-start
  8.6 1.4 %fusion = bf16[112,512]{1,0:T(8,128)(2,1)S(1)} fusion(bf16[2,512,512]{2,1,0:T(8,128)(2,1)} %param.4, bf16[112,1024]{1,0:T(8,128)(2,1)} %param.3), kind=kOutput, calls=%fused_computation.3 | convolution fusion | flops 59301888 | bytes 753664 | tf_op jit(solution)/shard_map/dot_general | solution.py:15
  10.0 0.7 %pad_maximum_fusion = bf16[112,1024]{1,0:T(8,128)(2,1)} fusion(bf16[112,512]{1,0:T(8,128)(2,1)S(1)} %fusion.1, bf16[112,512]{1,0:T(8,128)(2,1)S(1)} %fusion), kind=kLoop, calls=%fused_computation.14 | loop fusion | flops 458752 | bytes 458752 | tf_op jit(solution)/shard_map/concatenate | solution.py:19
  10.7 0.0 all-gather.2.cloned.1.call-update
  10.7 23.0 %all_gather.7 = bf16[448,1024]{1,0:T(8,128)(2,1)S(1)} all-gather(bf16[112,1024]{1,0:T(8,128)(2,1)} %pad_maximum_fusion), channel_id=1, replica_groups=mesh['row'=4,'col'=8] {'row'}, dimensions={0}, use_global_device_ids=true | all-gather | bytes 1146880 | tf_op jit(solution)/shard_map/all_gather | solution.py:20
  33.7 6.6 %all-gather.2.cloned.1.call-done = bf16[896,1024]{1,0:T(8,128)(2,1)} async-done(((bf16[112,1024]{1,0:T(8,128)(2,1)}), bf16[896,1024]{1,0:T(8,128)(2,1)}) %all-gather.2.cloned.1.call-update) | async-done | bytes 1835024 | tf_op jit(solution)/shard_map/all_gather | solution.py:22
  40.3 0.0 copy-done
  40.3 3.5 %subtract_convert_fusion = bf16[896,448]{0,1:T(8,128)(2,1)} fusion(bf16[896,448]{0,1:T(8,128)(2,1)S(1)} %copy-done, bf16[896,1024]{1,0:T(8,128)(2,1)} %all-gather.2.cloned.1.call-done, bf16[448,1024]{1,0:T(8,128)(2,1)S(1)} %all_gather.7), kind=kOutput, calls=%fused_computation | convolution fusion | flops 823287808 | bytes 4358144 | tf_op jit(solution)/shard_map/dot_general | solution.py:21
Async XLA Ops:
  7.2 33.1 %all-gather.2.cloned.1.call-start = ((), (), s32[]{:S(2)}) async-start(), calls=%async_computation | async-start | bytes 2064384 | tf_op jit(solution)/shard_map/all_gather | solution.py:22
  8.6 31.7 %copy-start = (bf16[896,448]{0,1:T(8,128)(2,1)S(1)}, bf16[896,448]{0,1:T(8,128)(2,1)}, u32[]{:S(2)}) copy-start(bf16[896,448]{0,1:T(8,128)(2,1)} %param.5) | copy-start | bytes 2408452
Sparse Core Ops, SparseCore 0:
  10.8 29.3 all-gather.1
where the time goes:
time: 50.9 us; the launch traced here: 50.7 us
  blocking collectives  23 us (45%)
  between operations  14.1 us (28%)
  waiting for transfers between devices  6.61 us (13%)
  matrix products  6.29 us (12%)
  other arithmetic  0.71 us (1%)
    all_gather x1, blocking collectives, body(): column_block = lax.all_gather(factor, 'row', axis=0, tiled=True)  23 us
    all_gather x1, waiting for transfers between devices, body(): lax.all_gather(factor, 'col', axis=0, tiled=True)  6.59 us
    dot_general x1, matrix products, body(): lax.dot_general(lax.all_gather(factor, 'col', axis=0, tiled=True), column...  3.54 us
    dot_general x2, matrix products, body(): jnp.dot(columns, jnp.tril(diag_inverse[panel]).T, preferred_element_type=...  2.75 us
  transfers between devices with their start and end apart: 1, of which 1 were waited for; matrix products, arithmetic and copies ran while one was open for 0% of the time, Pallas kernels for 0%

commit v1 on v0

--- a/solution.py
+++ b/solution.py
@@ -5,6 +5,18 @@
 
 NB = 512
 PANELS = 2
+
+
+def doubled_up(value, axis, dim):
+    ways, here = (lax.axis_size(axis), lax.axis_index(axis))
+    grown, reach = (value, 1)
+    while reach < ways:
+        theirs = lax.ppermute(grown, axis, [(d, d ^ reach) for d in range(ways)])
+        mine_first = jnp.concatenate([grown, theirs], axis=dim)
+        theirs_first = jnp.concatenate([theirs, grown], axis=dim)
+        grown = jnp.where(here & reach == 0, mine_first, theirs_first)
+        reach = 2 * reach
+    return grown
 
 
 def body(panel_block, diag_inverse, trailing):
@@ -19,7 +31,7 @@
     factor = jnp.concatenate(pieces, axis=1)
     column_block = lax.all_gather(factor, "row", axis=0, tiled=True)
     product = lax.dot_general(
-        lax.all_gather(factor, "col", axis=0, tiled=True),
+        doubled_up(factor, "col", 0),
         column_block,
         (((1,), (1,)), ((), ())),
         preferred_element_type=jnp.float32,

time: 50.9 us -> 43.7 us (0.86)
  between operations: 14.1 us -> 0.71 us
  waiting for transfers between devices: 6.61 us -> 11.9 us
  starting transfers between devices: 0.04 us -> 5.31 us
  matrix products: 6.29 us -> 3.79 us
  blocking collectives: 23 us -> 21.3 us
    ppermute x0 -> x3, waiting for transfers between devices: none -> 11.9 us  [doubled_up(): theirs = lax.ppermute(grown, axis, [(d, d ^ reach) for d in range(ways)])]
    all_gather x1 -> x0, waiting for transfers between devices: 6.59 us -> none  [body(): lax.all_gather(factor, 'col', axis=0, tiled=True)]
    ppermute x0 -> x3, starting transfers between devices: none -> 5.31 us  [doubled_up(): theirs = lax.ppermute(grown, axis, [(d, d ^ reach) for d in range(ways)])]
    all_gather x1, blocking collectives: 23 us -> 21.3 us  [body(): column_block = lax.all_gather(factor, 'row', axis=0, tiled=True)]
    dot_general x1, matrix products: 3.54 us -> 2.07 us  [body(): lax.dot_general(doubled_up(factor, 'col', 0), column_block, (((1,), (1,))...]
    dot_general x2, matrix products: 2.75 us -> 1.72 us  [body(): jnp.dot(columns, jnp.tril(diag_inverse[panel]).T, preferred_element_type=...]
    concatenate x1, other arithmetic: 0.71 us -> 0.02 us  [body(): factor = jnp.concatenate(pieces, axis=1)]
  transfers between devices with their start and end apart: 1 -> 3, of which waited for: 1 -> 2; matrix products, arithmetic and copies ran while one was open for 0% -> 0% of each run, Pallas kernels for 0% -> 0%
where the time goes in v1:
time: 43.7 us; the launch traced here: 43.5 us
  blocking collectives  21.3 us (49%)
  waiting for transfers between devices  11.9 us (27%)
  starting transfers between devices  5.31 us (12%)
  matrix products  3.79 us (9%)
  between operations  0.71 us (2%)
  other arithmetic  0.48 us (1%)
    all_gather x1, blocking collectives, body(): column_block = lax.all_gather(factor, 'row', axis=0, tiled=True)  21.3 us
    ppermute x3, waiting for transfers between devices, doubled_up(): theirs = lax.ppermute(grown, axis, [(d, d ^ reach) for d in range(ways)])  11.9 us
    ppermute x3, starting transfers between devices, doubled_up(): theirs = lax.ppermute(grown, axis, [(d, d ^ reach) for d in range(ways)])  5.31 us
    dot_general x1, matrix products, body(): lax.dot_general(doubled_up(factor, 'col', 0), column_block, (((1,), (1,))...  2.07 us
    dot_general x2, matrix products, body(): jnp.dot(columns, jnp.tril(diag_inverse[panel]).T, preferred_element_type=...  1.72 us
  transfers between devices with their start and end apart: 3, of which 2 were waited for; matrix products, arithmetic and copies ran while one was open for 0% of the time, Pallas kernels for 0%

profile of v1, /device:TPU:0, one launch (start us, length us, event | category | flops | bytes accessed | tf_op | source)
XLA Modules:
  0.0 43.5 jit_solution(16403604282638373129)
XLA Ops:
  0.6 0.0 copy-start.1
  0.6 0.0 copy-start.3
  0.6 1.4 %fusion.8 = bf16[112,512]{1,0:T(8,128)(2,1)S(1)} fusion(bf16[2,512,512]{2,1,0:T(8,128)(2,1)} %param.4, bf16[112,1024]{1,0:T(8,128)(2,1)} %param.3), kind=kOutput, calls=%fused_computation.12 | convolution fusion | flops 59301888 | bytes 753664 | tf_op jit(solution)/shard_map/dot_general | solution.py:27
  2.1 0.0 copy-done.1
  2.1 0.0 copy-done.3
  2.1 0.3 fusion.7
  2.4 0.0 copy-start
  2.4 0.6 %collective-permute-start = (bf16[112,1024]{1,0:T(8,128)(2,1)S(1)}, bf16[112,1024]{1,0:T(8,128)(2,1)S(1)}, u32[]{:S(2)}, u32[]{:S(2)}) collective-permute-start(bf16[112,1024]{1,0:T(8,128)(2,1)S(1)} %pad_maximum_fusion), channel_id=1, source_target_pairs={{0,1},{1,0},{2,3},{3,2},{4,5},{5,4},{6,7},{7,6},{8,9},{9,8},{10,11... | collective-permute-start | bytes 688136 | tf_op jit(solution)/shard_map/ppermute | solution.py:14
  3.0 1.1 %collective-permute-done = bf16[112,1024]{1,0:T(8,128)(2,1)S(1)} collective-permute-done((bf16[112,1024]{1,0:T(8,128)(2,1)S(1)}, bf16[112,1024]{1,0:T(8,128)(2,1)S(1)}, u32[]{:S(2)}, u32[]{:S(2)}) %collective-permute-start) | collective-permute-done | bytes 229408 | tf_op jit(solution)/shard_map/ppermute | solution.py:14
  4.1 0.1 maximum_select_fusion.5
  4.2 2.9 %collective-permute-start.1 = (bf16[224,1024]{1,0:T(8,128)(2,1)S(1)}, bf16[224,1024]{1,0:T(8,128)(2,1)S(1)}, u32[]{:S(2)}, u32[]{:S(2)}) collective-permute-start(bf16[224,1024]{1,0:T(8,128)(2,1)S(1)} %maximum_select_fusion.5), channel_id=1, source_target_pairs={{0,2},{1,3},{2,0},{3,1},{4,6},{5,7},{6,4},{7,5},{8,10},{9,11},{10,... | collective-permute-start | bytes 1376264 | tf_op jit(solution)/shard_map/ppermute | solution.py:14
  7.1 0.0 copy-start.2
  7.1 10.8 %collective-permute-done.1 = bf16[224,1024]{1,0:T(8,128)(2,1)S(1)} collective-permute-done((bf16[224,1024]{1,0:T(8,128)(2,1)S(1)}, bf16[224,1024]{1,0:T(8,128)(2,1)S(1)}, u32[]{:S(2)}, u32[]{:S(2)}) %collective-permute-start.1) | collective-permute-done | bytes 458784 | tf_op jit(solution)/shard_map/ppermute | solution.py:14
  18.0 0.4 maximum_select_fusion.4
  18.3 1.8 %collective-permute-start.2 = (bf16[448,1024]{1,0:T(8,128)(2,1)S(1)}, bf16[448,1024]{1,0:T(8,128)(2,1)S(1)}, u32[]{:S(2)}, u32[]{:S(2)}) collective-permute-start(bf16[448,1024]{1,0:T(8,128)(2,1)S(1)} %maximum_select_fusion.4), channel_id=1, source_target_pairs={{0,4},{1,5},{2,6},{3,7},{4,0},{5,1},{6,2},{7,3},{8,12},{9,13},{10,... | collective-permute-start | bytes 2752520 | tf_op jit(solution)/shard_map/ppermute | solution.py:14
  20.2 0.0 copy-done
  20.2 21.3 %all_gather.3 = bf16[448,1024]{1,0:T(8,128)(2,1)S(1)} all-gather(bf16[112,1024]{1,0:T(8,128)(2,1)S(1)} %pad_maximum_fusion), channel_id=1, replica_groups=mesh['row'=4,'col'=8] {'row'}, dimensions={0}, use_global_device_ids=true | all-gather | bytes 1146880 | tf_op jit(solution)/shard_map/all_gather | solution.py:32
  41.4 0.0 collective-permute-done.2
  41.4 0.0 copy-done.2
  41.4 2.1 %subtract_convert_fusion = bf16[896,448]{0,1:T(8,128)(2,1)} fusion(bf16[896,448]{0,1:T(8,128)(2,1)S(1)} %copy-done.2, bf16[448,1024]{1,0:T(8,128)(2,1)S(1)} %all_gather.3, bf16[448,1024]{1,0:T(8,128)(2,1)S(1)} %collective-permute-done.2, bf16[448,1024]{1,0:T(8,128)(2,1)S(1)} %maximum_select_fusion.4, pred[]{:T(512)S(6)} %eq.9), kind=kOutput, calls=%fused_computation.8 | convolution fusion | flops 831545344 | bytes 4358145 | tf_op jit(solution)/shard_map/dot_general | solution.py:33
  (1 shorter events, 0.0 us)
Async XLA Ops:
  0.6 1.5 %copy-start.1 = (bf16[2,512,512]{2,1,0:T(8,128)(2,1)S(1)}, bf16[2,512,512]{2,1,0:T(8,128)(2,1)}, u32[]{:S(2)}) copy-start(bf16[2,512,512]{2,1,0:T(8,128)(2,1)} %param.4) | copy-start | bytes 3145732
  0.6 1.5 %copy-start.3 = (bf16[112,1024]{1,0:T(8,128)(2,1)S(1)}, bf16[112,1024]{1,0:T(8,128)(2,1)}, u32[]{:S(2)}) copy-start(bf16[112,1024]{1,0:T(8,128)(2,1)} %param.3) | copy-start | bytes 688132
  2.4 17.7 %copy-start = (bf16[112,1024]{1,0:T(8,128)(2,1)}, bf16[112,1024]{1,0:T(8,128)(2,1)S(1)}, u32[]{:S(2)}) copy-start(bf16[112,1024]{1,0:T(8,128)(2,1)S(1)} %pad_maximum_fusion) | copy-start | bytes 688132
  2.4 1.7 %collective-permute-start = (bf16[112,1024]{1,0:T(8,128)(2,1)S(1)}, bf16[112,1024]{1,0:T(8,128)(2,1)S(1)}, u32[]{:S(2)}, u32[]{:S(2)}) collective-permute-start(bf16[112,1024]{1,0:T(8,128)(2,1)S(1)} %pad_maximum_fusion), channel_id=1, source_target_pairs={{0,1},{1,0},{2,3},{3,2},{4,5},{5,4},{6,7},{7,6},{8,9},{9,8},{10,11... | collective-permute-start | bytes 688136 | tf_op jit(solution)/shard_map/ppermute | solution.py:14
  4.2 13.7 %collective-permute-start.1 = (bf16[224,1024]{1,0:T(8,128)(2,1)S(1)}, bf16[224,1024]{1,0:T(8,128)(2,1)S(1)}, u32[]{:S(2)}, u32[]{:S(2)}) collective-permute-start(bf16[224,1024]{1,0:T(8,128)(2,1)S(1)} %maximum_select_fusion.5), channel_id=1, source_target_pairs={{0,2},{1,3},{2,0},{3,1},{4,6},{5,7},{6,4},{7,5},{8,10},{9,11},{10,... | collective-permute-start | bytes 1376264 | tf_op jit(solution)/shard_map/ppermute | solution.py:14
  7.1 34.3 %copy-start.2 = (bf16[896,448]{0,1:T(8,128)(2,1)S(1)}, bf16[896,448]{0,1:T(8,128)(2,1)}, u32[]{:S(2)}) copy-start(bf16[896,448]{0,1:T(8,128)(2,1)} %param.5) | copy-start | bytes 2408452
  18.3 23.1 %collective-permute-start.2 = (bf16[448,1024]{1,0:T(8,128)(2,1)S(1)}, bf16[448,1024]{1,0:T(8,128)(2,1)S(1)}, u32[]{:S(2)}, u32[]{:S(2)}) collective-permute-start(bf16[448,1024]{1,0:T(8,128)(2,1)S(1)} %maximum_select_fusion.4), channel_id=1, source_target_pairs={{0,4},{1,5},{2,6},{3,7},{4,0},{5,1},{6,2},{7,3},{8,12},{9,13},{10,... | collective-permute-start | bytes 2752520 | tf_op jit(solution)/shard_map/ppermute | solution.py:14
